TPU v7x, 32 devices: a whole 2x2x4 slice. The times are simulated.
32 devices in a mesh: chi: 4 (over y, x), dl: 4 (over z), cell: 2 (over core).
Axes of the slice: x: 2, y: 2, z: 4, core: 2. Of those that a mesh axis runs over, the one named last changes fastest.
Arguments:
- left_env: bfloat16 [2, 512, 512, 36], P('cell', None, 'chi'), may hold values from -6 to 6
- up_left: bfloat16 [2, 512, 36, 512], P('cell', 'chi', None, 'dl'), may hold values from -0.109375 to 0.109375
- up_center: bfloat16 [2, 512, 36, 512], P('cell', 'chi', None, 'dl'), may hold values from -0.109375 to 0.109375
- right_env: bfloat16 [2, 512, 36, 512], P('cell', 'dl'), may hold values from -0.046875 to 0.046875
- center: bfloat16 [2, 512, 512], P('cell', None, 'dl'), may hold values from -0.25 to 0.25
- ket_tensor: bfloat16 [2, 6, 6, 6, 6, 2], P('cell'), may hold values from -0.875 to 0.875
Outputs:
- left_env_new: float32 [2, 512, 36, 512], P('cell', 'chi', None, 'dl')
- new_left: float32 [2, 512, 36, 512], P('cell', 'chi', None, 'dl')
All inputs are finite; a program needn't handle non-finite values.
Results may differ from a plain program's by a relative error of at most 0.0066.
The roundings to bfloat16 on the way count: a program that leaves them out, or rounds other values in their place, can miss the bound.
Values may be sent and summed in bfloat16 or wider, within the bound.
A program may use at most 256 MiB of HBM per device.

v0:
```python
from functools import partial
import math
import jax
import jax.numpy as jnp
from jax import lax
from jax.sharding import PartitionSpec as P

ITERS = 5
HIGHEST = lax.Precision.HIGHEST


def from_behind(block, axis, distance):
    devices = range(lax.axis_size(axis))
    route = [((i - distance) % len(devices), i) for i in devices]
    return lax.ppermute(block, axis, route)


def layered(block, tensor):
    leg_size = tensor.shape[0]
    amount = block.shape[0]
    columns = block.shape[3]
    unfolded = block.reshape(amount, leg_size, leg_size, leg_size, leg_size, columns)
    ket_side = jnp.einsum(
        "blLuUc,lurdp->bLUcrdp", unfolded, tensor, preferred_element_type=jnp.float32
    ).astype(jnp.bfloat16)
    both_sides = jnp.einsum(
        "bLUcrdp,LUsep->brsdec", ket_side, tensor, preferred_element_type=jnp.float32
    )
    return both_sides.reshape(amount, leg_size * leg_size, leg_size * leg_size, columns).astype(
        jnp.bfloat16
    )


def through_site(stacked, tensor):
    amount = stacked.shape[0]
    stride = min(amount, 8)
    blocks = stacked.reshape((amount // stride, stride) + stacked.shape[1:])
    finished = lax.map(partial(layered, tensor=tensor), blocks)
    return finished.reshape((amount,) + finished.shape[2:])


def shards(left_env, up_left, up_center, right_env, center, ket_tensor):
    env_local = left_env[0]
    left_iso = up_left[0]
    left_mid = up_center[0]
    env_right = right_env[0]
    bond_mat = center[0]
    site_ket = ket_tensor[0]
    chi_all = env_local.shape[0]
    leg_width = env_local.shape[2]
    col_count = left_iso.shape[2]
    iso_all, mid_all = (
        lax.all_gather(left_iso, "chi", axis=0, tiled=True),
        lax.all_gather(left_mid, "chi", axis=0, tiled=True),
    )
    left_sum = jnp.einsum("abm,asc->bmsc", env_local, iso_all, preferred_element_type=jnp.float32)
    left_cut = through_site(left_sum.astype(jnp.bfloat16), site_ket)
    right_sum = jnp.einsum("abm,asc->bmsc", env_local, mid_all, preferred_element_type=jnp.float32)
    right_cut = through_site(right_sum.astype(jnp.bfloat16), site_ket)
    next_iso = from_behind(left_iso, "cell", -1)
    bra_iso = lax.all_gather(next_iso, "dl", axis=2, tiled=True)
    env_new = lax.psum_scatter(
        jnp.einsum("bmdc,bdk->kmc", left_cut, bra_iso, preferred_element_type=jnp.float32),
        "chi",
        scatter_dimension=0,
        tiled=True,
    )
    center_term = jnp.einsum(
        "bmda,amc->cbd", right_cut, env_right, preferred_element_type=jnp.float32
    )
    mixed = jnp.einsum(
        "abm,ax->bmx", env_local, bond_mat, preferred_element_type=jnp.float32
    ).astype(jnp.bfloat16)
    bond_term = jnp.einsum("bma,amc->cb", mixed, env_right, preferred_element_type=jnp.float32)
    center_part, bond_part = (
        lax.psum_scatter(center_term, "dl", scatter_dimension=0, tiled=True),
        lax.psum_scatter(bond_term, "dl", scatter_dimension=0, tiled=True),
    )
    center_all, bond_cols = (
        lax.all_gather(center_part.astype(jnp.bfloat16), "dl", axis=0, tiled=True),
        lax.all_gather(bond_part.astype(jnp.bfloat16), "dl", axis=0, tiled=True),
    )
    bond_full = lax.all_gather(bond_cols, "chi", axis=1, tiled=True)
    bond_mine = lax.dynamic_slice_in_dim(bond_full, lax.axis_index("dl") * col_count, col_count, 1)
    target = jnp.einsum("cbd,cx->bdx", center_all, bond_mine, preferred_element_type=jnp.float32)
    factor = 0.25 * math.sqrt(chi_all)
    norm_sum = lax.psum(jnp.sum(target * target), ("chi", "dl"))
    current = target * (factor / jnp.sqrt(norm_sum))
    for sweep_index in range(ITERS):
        spread = lax.all_gather(current.astype(jnp.bfloat16), "dl", axis=2, tiled=True).astype(
            current.dtype
        )
        gram_rows = lax.psum(
            jnp.einsum("bdx,bdy->xy", current, spread, precision=HIGHEST).astype(jnp.bfloat16),
            "chi",
        ).astype(jnp.float32)
        current = 1.5 * current - 0.5 * jnp.einsum(
            "bdy,xy->bdx", spread, gram_rows, precision=HIGHEST
        )
    new_left = current * math.sqrt(chi_all * leg_width)
    return (env_new[None], new_left[None])


def solution(mesh):
    placed = (
        P("cell", None, "chi", None),
        P("cell", "chi", None, "dl"),
        P("cell", "chi", None, "dl"),
        P("cell", "dl", None, None),
        P("cell", None, "dl"),
        P("cell", None, None, None, None, None),
    )
    return jax.shard_map(
        shards,
        mesh=mesh,
        in_specs=placed,
        out_specs=(P("cell", "chi", None, "dl"), P("cell", "chi", None, "dl")),
        check_vma=False,
    )
```

profile of v0, /device:TPU:0, one launch (start us, length us, event | category | flops | bytes accessed | tf_op | source)
XLA Modules:
  0.0 1720.3 jit_solution(1469185994787700763)
XLA Ops:
  9.4 60.3 %all-gather.28.cloned.1.call-done = bf16[1,512,36,128]{3,1,2,0:T(8,128)(2,1)} async-done(((bf16[1,128,36,128]{3,1,2,0:T(8,128)(2,1)}), bf16[1,512,36,128]{3,1,2,0:T(8,128)(2,1)}) %all-gather.28.cloned.1.call-update) | async-done | bytes 4718608 | tf_op jit(solution)/shard_map/all_gather | solution.py:54
  69.7 29.6 %convert_bitcast_fusion = bf16[16,8,36,36,128]{4,1,0,3,2:T(8,128)(2,1)} fusion(bf16[1,512,128,36]{2,1,3,0:T(8,128)(2,1)} %param.10, bf16[1,512,36,128]{3,1,2,0:T(8,128)(2,1)} %all-gather.28.cloned.1.call-done), kind=kOutput, calls=%fused_computation.26 | convolution fusion | flops 21764505600 | bytes 51904512 | tf_op jit(solution)/shard_map/abm,asc->bmsc/dot_general | solution.py:58
  99.2 14.1 broadcast.9.clone2.1
  113.3 220.6 %while.21 = (s32[]{:T(128)}, bf16[16,8,36,36,128]{4,1,0,3,2:T(8,128)(2,1)}, bf16[16,8,36,36,128]{4,1,0,3,2:T(8,128)(2,1)}, bf16[6,6,6,6,2]{1,3,4,0,2:T(8,128)(2,1)S(1)}, s32[]{:T(128)}) while((s32[]{:T(128)}, bf16[16,8,36,36,128]{4,1,0,3,2:T(8,128)(2,1)}, bf16[16,8,36,36,128]{4,1,0,3,2:T(8,128)(2,1)}, bf16[6,6,6,6,2]{1,3,4,0,2:T(8,128)(2,1)S(1)}, ...), condition=%wide.region_4.5_spmd, body=%wide.region_3.4_spmd.sunk | while | flops 386187264 | bytes 31861440 | solution.py:38
  334.0 28.7 %fusion.37 = f32[512,128,36]{0,1,2:T(8,128)} fusion(bf16[1,128,36,512]{3,1,2,0:T(8,128)(2,1)} %param.13, bf16[16,8,36,36,128]{4,1,0,3,2:T(8,128)(2,1)} %get-tuple-element.47), kind=kOutput, calls=%fused_computation.39 | convolution fusion | flops 21743271936 | bytes 56623104 | tf_op jit(solution)/shard_map/bmda,amc->cbd/dot_general | solution.py:68
  370.0 154.1 %reduce-scatter.6.cloned.1.call-done = f32[128,128,36]{0,1,2:T(8,128)} async-done(((f32[512,128,36]{0,1,2:T(8,128)}), f32[128,128,36]{0,1,2:T(8,128)}) %reduce-scatter.6.cloned.1.call-update) | async-done | bytes 2359312 | tf_op jit(solution)/shard_map/reduce_scatter | solution.py:76
  527.0 20.4 %reduce-scatter.8.cloned.1.call-done = f32[128,128]{0,1:T(8,128)} async-done(((f32[512,128]{0,1:T(8,128)}), f32[128,128]{0,1:T(8,128)}) %reduce-scatter.8.cloned.1.call-update) | async-done | bytes 65552 | tf_op jit(solution)/shard_map/reduce_scatter | solution.py:77
  570.6 68.2 %all-gather.14.cloned.1.call-done = bf16[512,128,36]{0,1,2:T(8,128)(2,1)} async-done(((bf16[128,128,36]{0,1,2:T(8,128)(2,1)}), bf16[512,128,36]{0,1,2:T(8,128)(2,1)}) %all-gather.14.cloned.1.call-update) | async-done | bytes 4718608 | tf_op jit(solution)/shard_map/all_gather | solution.py:80
  643.1 38.9 %psum.42 = f32[]{:T(128)} all-reduce(f32[]{:T(128)} %get-tuple-element.94), channel_id=1, replica_groups=mesh['chi'=4,'dl'=4,'cell'=2] {'chi','dl'}, use_global_device_ids=true, to_apply=%region_8.9 | all-reduce | flops 1 | bytes 8 | tf_op jit(solution)/shard_map/psum | solution.py:87
  684.1 86.6 %all-gather.16.cloned.1.call-done = bf16[128,36,512]{2,0,1:T(8,128)(2,1)} async-done(((bf16[128,36,128]{2,0,1:T(8,128)(2,1)}), bf16[128,36,512]{2,0,1:T(8,128)(2,1)}) %all-gather.16.cloned.1.call-update) | async-done | bytes 4718608 | tf_op jit(solution)/shard_map/all_gather | solution.py:90
  776.2 40.3 %all-reduce.6.cloned.1.call-done = bf16[128,512]{1,0:T(8,128)(2,1)} async-done(((bf16[128,512]{1,0:T(8,128)(2,1)}), bf16[128,512]{1,0:T(8,128)(2,1)}) %all-reduce.6.cloned.1.call-update) | async-done | bytes 131088 | tf_op jit(solution)/shard_map/psum | solution.py:93
  822.3 89.0 %all-gather.18.cloned.1.call-done = bf16[128,36,512]{2,0,1:T(8,128)(2,1)} async-done(((bf16[128,36,128]{2,0,1:T(8,128)(2,1)}), bf16[128,36,512]{2,0,1:T(8,128)(2,1)}) %all-gather.18.cloned.1.call-update) | async-done | bytes 4718608 | tf_op jit(solution)/shard_map/all_gather | solution.py:90
  917.6 40.3 %all-reduce.8.cloned.1.call-done = bf16[128,512]{1,0:T(8,128)(2,1)} async-done(((bf16[128,512]{1,0:T(8,128)(2,1)}), bf16[128,512]{1,0:T(8,128)(2,1)}) %all-reduce.8.cloned.1.call-update) | async-done | bytes 131088 | tf_op jit(solution)/shard_map/psum | solution.py:93
  963.5 89.2 %all-gather.20.cloned.1.call-done = bf16[128,36,512]{2,0,1:T(8,128)(2,1)} async-done(((bf16[128,36,128]{2,0,1:T(8,128)(2,1)}), bf16[128,36,512]{2,0,1:T(8,128)(2,1)}) %all-gather.20.cloned.1.call-update) | async-done | bytes 4718608 | tf_op jit(solution)/shard_map/all_gather | solution.py:90
  1059.0 40.3 %all-reduce.10.cloned.1.call-done = bf16[128,512]{1,0:T(8,128)(2,1)} async-done(((bf16[128,512]{1,0:T(8,128)(2,1)}), bf16[128,512]{1,0:T(8,128)(2,1)}) %all-reduce.10.cloned.1.call-update) | async-done | bytes 131088 | tf_op jit(solution)/shard_map/psum | solution.py:93
  1105.6 88.6 %all-gather.22.cloned.1.call-done = bf16[128,36,512]{2,0,1:T(8,128)(2,1)} async-done(((bf16[128,36,128]{2,0,1:T(8,128)(2,1)}), bf16[128,36,512]{2,0,1:T(8,128)(2,1)}) %all-gather.22.cloned.1.call-update) | async-done | bytes 4718608 | tf_op jit(solution)/shard_map/all_gather | solution.py:90
  1200.7 50.5 %all-gather.26.cloned.1.call-done = bf16[1,512,36,128]{3,1,2,0:T(8,128)(2,1)} async-done(((bf16[1,128,36,128]{3,1,2,0:T(8,128)(2,1)}), bf16[1,512,36,128]{3,1,2,0:T(8,128)(2,1)}) %all-gather.26.cloned.1.call-update) | async-done | bytes 4718608 | tf_op jit(solution)/shard_map/all_gather | solution.py:53
  1251.1 29.6 %convert_bitcast_fusion.1 = bf16[16,8,36,36,128]{4,1,0,3,2:T(8,128)(2,1)} fusion(bf16[1,512,128,36]{2,1,3,0:T(8,128)(2,1)} %param.10, bf16[1,512,36,128]{3,1,2,0:T(8,128)(2,1)} %all-gather.26.cloned.1.call-done), kind=kOutput, calls=%fused_computation.27 | convolution fusion | flops 21764505600 | bytes 51904512 | tf_op jit(solution)/shard_map/abm,asc->bmsc/dot_general | solution.py:56
  1280.7 15.9 all-reduce.12.cloned.1.call-done
  1302.4 14.7 broadcast.9.clone2
  1317.1 220.8 %while.20 = (s32[]{:T(128)}, bf16[16,8,36,36,128]{4,1,0,3,2:T(8,128)(2,1)}, bf16[16,8,36,36,128]{4,1,0,3,2:T(8,128)(2,1)}, bf16[6,6,6,6,2]{1,3,4,0,2:T(8,128)(2,1)S(1)}, s32[]{:T(128)}) while((s32[]{:T(128)}, bf16[16,8,36,36,128]{4,1,0,3,2:T(8,128)(2,1)}, bf16[16,8,36,36,128]{4,1,0,3,2:T(8,128)(2,1)}, bf16[6,6,6,6,2]{1,3,4,0,2:T(8,128)(2,1)S(1)}, ...), condition=%wide.region_1.2_spmd, body=%wide.region_0.1_spmd.sunk | while | flops 386187264 | bytes 31861440 | solution.py:38
  1537.9 29.8 %fusion.32 = f32[512,36,128]{0,2,1:T(8,128)} fusion(bf16[128,36,512]{2,0,1:T(8,128)(2,1)} %all-gather.12.cloned.1.call-done, bf16[16,8,36,36,128]{4,1,0,3,2:T(8,128)(2,1)} %get-tuple-element.46), kind=kOutput, calls=%fused_computation.38 | convolution fusion | flops 21743271936 | bytes 56623104 | tf_op jit(solution)/shard_map/bmdc,bdk->kmc/dot_general | solution.py:63
  1574.8 88.0 %reduce-scatter.4.cloned.1.call-done = f32[128,36,128]{0,2,1:T(8,128)} async-done(((f32[512,36,128]{0,2,1:T(8,128)}), f32[128,36,128]{0,2,1:T(8,128)}) %reduce-scatter.4.cloned.1.call-update) | async-done | bytes 2359312 | tf_op jit(solution)/shard_map/reduce_scatter | solution.py:62
  1665.9 42.5 %all-reduce.14.cloned.1.call-done = bf16[128,512]{1,0:T(8,128)(2,1)} async-done(((bf16[128,512]{1,0:T(8,128)(2,1)}), bf16[128,512]{1,0:T(8,128)(2,1)}) %all-reduce.14.cloned.1.call-update) | async-done | bytes 131088 | tf_op jit(solution)/shard_map/psum | solution.py:93
  (225 shorter events, 545.1 us)
Async XLA Ops:
  7.2 355.5 %copy-start = (bf16[1,512,128]{2,1,0:T(8,128)(2,1)S(1)}, bf16[1,512,128]{2,1,0:T(8,128)(2,1)}, u32[]{:S(2)}) copy-start(bf16[1,512,128]{2,1,0:T(8,128)(2,1)} %param.14) | copy-start | bytes 393220
  7.2 62.5 %all-gather.28.cloned.1.call-start = ((), (), s32[]{:S(2)}) async-start(), calls=%async_computation.19 | async-start | bytes 5898240 | tf_op jit(solution)/shard_map/all_gather | solution.py:54
  7.9 516.2 %reduce-scatter.6.cloned.1.call-start = ((), (), s32[]{:S(2)}) async-start(), calls=%async_computation.5 | async-start | bytes 11796480 | tf_op jit(solution)/shard_map/reduce_scatter | solution.py:76
  362.6 184.8 %reduce-scatter.8.cloned.1.call-start = ((), (), s32[]{:S(2)}) async-start(), calls=%async_computation.7 | async-start | bytes 327680 | tf_op jit(solution)/shard_map/reduce_scatter | solution.py:77
  370.0 268.8 %all-gather.14.cloned.1.call-start = ((), (), s32[]{:S(2)}) async-start(), calls=%async_computation.6 | async-start | bytes 5898240 | tf_op jit(solution)/shard_map/all_gather | solution.py:80
  527.0 243.7 %all-gather.16.cloned.1.call-start = ((), (), s32[]{:S(2)}) async-start(), calls=%async_computation.8 | async-start | bytes 5898240 | tf_op jit(solution)/shard_map/all_gather | solution.py:90
  684.1 132.4 %all-reduce.6.cloned.1.call-start = ((), (), s32[]{:S(2)}) async-start(), calls=%async_computation.9 | async-start | bytes 262144 | tf_op jit(solution)/shard_map/psum | solution.py:93
  776.2 135.2 %all-gather.18.cloned.1.call-start = ((), (), s32[]{:S(2)}) async-start(), calls=%async_computation.10 | async-start | bytes 5898240 | tf_op jit(solution)/shard_map/all_gather | solution.py:90
  822.1 135.9 %copy-start.3 = (f32[128,36,128]{2,0,1:T(8,128)S(1)}, f32[128,36,128]{2,0,1:T(8,128)}, u32[]{:S(2)}) copy-start(f32[128,36,128]{2,0,1:T(8,128)} %get-tuple-element.97) | copy-start | bytes 7077892
  822.1 135.8 %all-reduce.8.cloned.1.call-start = ((), (), s32[]{:S(2)}) async-start(), calls=%async_computation.11 | async-start | bytes 262144 | tf_op jit(solution)/shard_map/psum | solution.py:93
  917.6 135.2 %all-gather.20.cloned.1.call-start = ((), (), s32[]{:S(2)}) async-start(), calls=%async_computation.12 | async-start | bytes 5898240 | tf_op jit(solution)/shard_map/all_gather | solution.py:90
  963.5 135.8 %all-reduce.10.cloned.1.call-start = ((), (), s32[]{:S(2)}) async-start(), calls=%async_computation.13 | async-start | bytes 262144 | tf_op jit(solution)/shard_map/psum | solution.py:93
  1058.9 135.2 %all-gather.22.cloned.1.call-start = ((), (), s32[]{:S(2)}) async-start(), calls=%async_computation.14 | async-start | bytes 5898240 | tf_op jit(solution)/shard_map/all_gather | solution.py:90
  1104.9 146.3 %all-gather.26.cloned.1.call-start = ((), (), s32[]{:S(2)}) async-start(), calls=%async_computation.18 | async-start | bytes 5898240 | tf_op jit(solution)/shard_map/all_gather | solution.py:53
  1105.4 191.2 %all-reduce.12.cloned.1.call-start = ((), (), s32[]{:S(2)}) async-start(), calls=%async_computation.15 | async-start | bytes 262144 | tf_op jit(solution)/shard_map/psum | solution.py:93
  1105.5 94.2 %collective-permute-start = (bf16[128,36,128]{2,0,1:T(8,128)(2,1)}, bf16[128,36,128]{2,0,1:T(8,128)(2,1)}, u32[]{:S(2)}, u32[]{:S(2)}) collective-permute-start(bf16[128,36,128]{2,0,1:T(8,128)(2,1)} %bitcast.242), channel_id=1, source_target_pairs={{1,0},{0,1},{3,2},{2,3},{5,4},{4,5},{7,6},{6,7},{9,8},{8,9},{11,10... | collective-permute-start | bytes 3538952 | tf_op jit(solution)/shard_map/ppermute | solution.py:15
  1199.6 338.3 %all-gather.12.cloned.1.call-start = ((), (), s32[]{:S(2)}) async-start(), calls=%async_computation.3 | async-start | bytes 5898240 | tf_op jit(solution)/shard_map/all_gather | solution.py:61
  1200.2 367.8 %all-gather.24.cloned.1.call-start = ((), (), s32[]{:S(2)}) async-start(), calls=%async_computation.16 | async-start | bytes 5898240 | tf_op jit(solution)/shard_map/all_gather | solution.py:90
  1302.2 360.7 %reduce-scatter.4.cloned.1.call-start = ((), (), s32[]{:S(2)}) async-start(), calls=%async_computation.4 | async-start | bytes 11796480 | tf_op jit(solution)/shard_map/reduce_scatter | solution.py:62
  1567.7 1.7 copy-start.2
  1567.7 140.7 %all-reduce.14.cloned.1.call-start = ((), (), s32[]{:S(2)}) async-start(), calls=%async_computation.17 | async-start | bytes 262144 | tf_op jit(solution)/shard_map/psum | solution.py:93
  1662.8 50.7 %copy-start.1 = (bf16[1,512,128]{2,1,0:T(8,128)(2,1)S(1)}, bf16[1,512,128]{2,1,0:T(8,128)(2,1)}, u32[]{:S(2)}) copy-start(bf16[1,512,128]{2,1,0:T(8,128)(2,1)} %param.14) | copy-start | bytes 393220
Sparse Core Ops, SparseCore 0:
  9.9 59.7 all-gather.27
  362.8 161.2 reduce-scatter.5
  526.9 20.4 reduce-scatter.7
  549.5 89.1 all-gather.13
  684.2 86.4 all-gather.15
  776.3 40.1 all-reduce.5
  822.2 89.1 all-gather.17
  917.7 40.1 all-reduce.7
  963.6 89.1 all-gather.19
  1059.1 40.1 all-reduce.9
  1105.0 89.1 all-gather.21
  1195.8 55.2 all-gather.25
  1254.6 41.9 all-reduce.11
  1298.1 89.1 all-gather.11
  1389.3 87.3 all-gather.23
  1567.8 94.9 reduce-scatter.3
  1666.4 41.9 all-reduce.13
where the time goes:
time: 1730 us; the launch traced here: 1720 us
  waiting for transfers between devices  976 us (56%)
  matrix products  408 us (24%)
  local copies, waits for them, and re-layouts  252 us (15%)
  blocking collectives  61.2 us (4%)
    all_gather x5, waiting for transfers between devices, shards(): lax.all_gather(current.astype(jnp.bfloat16), 'dl', axis=2, tiled=True)  353 us
    psum x5, waiting for transfers between devices, shards(): lax.psum(jnp.einsum('bdx,bdy->xy', current, spread, precision=HIGHEST).as...  179 us
    reduce_scatter x1, waiting for transfers between devices, shards(): lax.psum_scatter(center_term, 'dl', scatter_dimension=0, tiled=True)  154 us
    dot_general x32, matrix products, layered(): jnp.einsum('bLUcrdp,LUsep->brsdec', ket_side, tensor, preferred_element_t...  138 us
    convert_element_type x32, local copies, waits for them, and re-layouts, layered(): both_sides.reshape(amount, leg_size * leg_size, leg_size * leg_size, colu...  98.5 us
    reduce_scatter x1, waiting for transfers between devices, shards(): lax.psum_scatter(jnp.einsum('bmdc,bdk->kmc', left_cut, bra_iso, preferred...  88 us
    dot_general x32, matrix products, layered(): jnp.einsum('blLuUc,lurdp->bLUcrdp', unfolded, tensor, preferred_element_t...  84.9 us
    all_gather x1, waiting for transfers between devices, shards(): lax.all_gather(center_part.astype(jnp.bfloat16), 'dl', axis=0, tiled=True)  68.2 us
  transfers between devices with their start and end apart: 18, of which 15 were waited for; matrix products, arithmetic and copies ran while one was open for 19% of the time, Pallas kernels for 0%

commit v1 on v0

--- a/solution.py
+++ b/solution.py
@@ -90,7 +90,8 @@
         spread = lax.all_gather(current.astype(jnp.bfloat16), "dl", axis=2, tiled=True).astype(
             current.dtype
         )
-        gram_rows = lax.psum(
+        feed_meshes = lambda load, chip_axis: jnp.sum(lax.all_gather(load, chip_axis), axis=0)
+        gram_rows = feed_meshes(
             jnp.einsum("bdx,bdy->xy", current, spread, precision=HIGHEST).astype(jnp.bfloat16),
             "chi",
         ).astype(jnp.float32)

time: 1730 us -> 1540 us (0.89)
  waiting for transfers between devices: 976 us -> 718 us
  blocking collectives: 61.2 us -> 121 us
    psum x5 -> x0, waiting for transfers between devices: 179 us -> none  [shards(): lax.psum(jnp.einsum('bdx,bdy->xy', current, spread, precision=HIGHEST).as...]
    all_gather x0 -> x5, blocking collectives: none -> 59.8 us  [shards(): lax.all_gather(load, chip_axis)]
    all_gather x5, waiting for transfers between devices: 353 us -> 312 us  [shards(): lax.all_gather(current.astype(jnp.bfloat16), 'dl', axis=2, tiled=True)]
    all_gather x1, waiting for transfers between devices: 50.5 us -> 29 us  [shards(): lax.all_gather(left_iso, 'chi', axis=0, tiled=True)]
    reduce_scatter x1, waiting for transfers between devices: 88 us -> 69.6 us  [shards(): lax.psum_scatter(jnp.einsum('bmdc,bdk->kmc', left_cut, bra_iso, preferred...]
  transfers between devices with their start and end apart: 18 -> 13, of which waited for: 15 -> 11; matrix products, arithmetic and copies ran while one was open for 19% -> 22% of each run, Pallas kernels for 0% -> 0%
where the time goes in v1:
time: 1540 us; the launch traced here: 1530 us
  waiting for transfers between devices  718 us (47%)
  matrix products  404 us (26%)
  local copies, waits for them, and re-layouts  252 us (16%)
  blocking collectives  121 us (8%)
  between operations  15.4 us (1%)
    all_gather x5, waiting for transfers between devices, shards(): lax.all_gather(current.astype(jnp.bfloat16), 'dl', axis=2, tiled=True)  312 us
    reduce_scatter x1, waiting for transfers between devices, shards(): lax.psum_scatter(center_term, 'dl', scatter_dimension=0, tiled=True)  154 us
    dot_general x32, matrix products, layered(): jnp.einsum('bLUcrdp,LUsep->brsdec', ket_side, tensor, preferred_element_t...  138 us
    convert_element_type x32, local copies, waits for them, and re-layouts, layered(): both_sides.reshape(amount, leg_size * leg_size, leg_size * leg_size, colu...  98.5 us
    dot_general x32, matrix products, layered(): jnp.einsum('blLuUc,lurdp->bLUcrdp', unfolded, tensor, preferred_element_t...  85 us
    reduce_scatter x1, waiting for transfers between devices, shards(): lax.psum_scatter(jnp.einsum('bmdc,bdk->kmc', left_cut, bra_iso, preferred...  69.6 us
    all_gather x1, waiting for transfers between devices, shards(): lax.all_gather(center_part.astype(jnp.bfloat16), 'dl', axis=0, tiled=True)  68.1 us
    dynamic_slice x32, local copies, waits for them, and re-layouts, through_site(): finished = lax.map(partial(layered, tensor=tensor), blocks)  61.6 us
  transfers between devices with their start and end apart: 13, of which 11 were waited for; matrix products, arithmetic and copies ran while one was open for 22% of the time, Pallas kernels for 0%

profile of v1, /device:TPU:0, one launch (start us, length us, event | category | flops | bytes accessed | tf_op | source)
XLA Modules:
  0.0 1527.5 jit_solution(13196005107903824257)
XLA Ops:
  9.4 60.3 %all-gather.33.cloned.1.call-done = bf16[1,512,36,128]{3,1,2,0:T(8,128)(2,1)} async-done(((bf16[1,128,36,128]{3,1,2,0:T(8,128)(2,1)}), bf16[1,512,36,128]{3,1,2,0:T(8,128)(2,1)}) %all-gather.33.cloned.1.call-update) | async-done | bytes 4718608 | tf_op jit(solution)/shard_map/all_gather | solution.py:54
  69.7 29.5 %convert_bitcast_fusion = bf16[16,8,36,36,128]{4,1,0,3,2:T(8,128)(2,1)} fusion(bf16[1,512,128,36]{2,1,3,0:T(8,128)(2,1)} %param.10, bf16[1,512,36,128]{3,1,2,0:T(8,128)(2,1)} %all-gather.33.cloned.1.call-done), kind=kOutput, calls=%fused_computation.26 | convolution fusion | flops 21764505600 | bytes 51904512 | tf_op jit(solution)/shard_map/abm,asc->bmsc/dot_general | solution.py:58
  99.2 14.1 broadcast.9.clone2.1
  113.3 220.7 %while.21 = (s32[]{:T(128)}, bf16[16,8,36,36,128]{4,1,0,3,2:T(8,128)(2,1)}, bf16[16,8,36,36,128]{4,1,0,3,2:T(8,128)(2,1)}, bf16[6,6,6,6,2]{1,3,4,0,2:T(8,128)(2,1)S(1)}, s32[]{:T(128)}) while((s32[]{:T(128)}, bf16[16,8,36,36,128]{4,1,0,3,2:T(8,128)(2,1)}, bf16[16,8,36,36,128]{4,1,0,3,2:T(8,128)(2,1)}, bf16[6,6,6,6,2]{1,3,4,0,2:T(8,128)(2,1)S(1)}, ...), condition=%wide.region_4.5_spmd, body=%wide.region_3.4_spmd.sunk | while | flops 386187264 | bytes 31861440 | solution.py:38
  334.0 28.7 %fusion.37 = f32[512,128,36]{0,1,2:T(8,128)} fusion(bf16[1,128,36,512]{3,1,2,0:T(8,128)(2,1)} %param.13, bf16[16,8,36,36,128]{4,1,0,3,2:T(8,128)(2,1)} %get-tuple-element.47), kind=kOutput, calls=%fused_computation.39 | convolution fusion | flops 21743271936 | bytes 56623104 | tf_op jit(solution)/shard_map/bmda,amc->cbd/dot_general | solution.py:68
  370.1 154.1 %reduce-scatter.6.cloned.1.call-done = f32[128,128,36]{0,1,2:T(8,128)} async-done(((f32[512,128,36]{0,1,2:T(8,128)}), f32[128,128,36]{0,1,2:T(8,128)}) %reduce-scatter.6.cloned.1.call-update) | async-done | bytes 2359312 | tf_op jit(solution)/shard_map/reduce_scatter | solution.py:76
  527.1 20.4 %reduce-scatter.8.cloned.1.call-done = f32[128,128]{0,1:T(8,128)} async-done(((f32[512,128]{0,1:T(8,128)}), f32[128,128]{0,1:T(8,128)}) %reduce-scatter.8.cloned.1.call-update) | async-done | bytes 65552 | tf_op jit(solution)/shard_map/reduce_scatter | solution.py:77
  548.4 12.3 all_gather.67
  560.7 10.0 all_gather.68
  570.7 68.1 %all-gather.19.cloned.1.call-done = bf16[512,128,36]{0,1,2:T(8,128)(2,1)} async-done(((bf16[128,128,36]{0,1,2:T(8,128)(2,1)}), bf16[512,128,36]{0,1,2:T(8,128)(2,1)}) %all-gather.19.cloned.1.call-update) | async-done | bytes 4718608 | tf_op jit(solution)/shard_map/all_gather | solution.py:80
  643.2 38.9 %psum.7 = f32[]{:T(128)} all-reduce(f32[]{:T(128)} %get-tuple-element.94), channel_id=1, replica_groups=mesh['chi'=4,'dl'=4,'cell'=2] {'chi','dl'}, use_global_device_ids=true, to_apply=%region_8.9 | all-reduce | flops 1 | bytes 8 | tf_op jit(solution)/shard_map/psum | solution.py:87
  684.2 86.6 %all-gather.21.cloned.1.call-done = bf16[128,36,512]{2,0,1:T(8,128)(2,1)} async-done(((bf16[128,36,128]{2,0,1:T(8,128)(2,1)}), bf16[128,36,512]{2,0,1:T(8,128)(2,1)}) %all-gather.21.cloned.1.call-update) | async-done | bytes 4718608 | tf_op jit(solution)/shard_map/all_gather | solution.py:90
  792.0 10.0 all-gather.25.cloned.1.call-start
  802.0 75.8 %all-gather.23.cloned.1.call-done = bf16[128,36,512]{2,0,1:T(8,128)(2,1)} async-done(((bf16[128,36,128]{2,0,1:T(8,128)(2,1)}), bf16[128,36,512]{2,0,1:T(8,128)(2,1)}) %all-gather.23.cloned.1.call-update) | async-done | bytes 4718608 | tf_op jit(solution)/shard_map/all_gather | solution.py:90
  883.3 15.0 all-gather.3
  907.3 29.0 %all-gather.31.cloned.1.call-done = bf16[1,512,36,128]{3,1,2,0:T(8,128)(2,1)} async-done(((bf16[1,128,36,128]{3,1,2,0:T(8,128)(2,1)}), bf16[1,512,36,128]{3,1,2,0:T(8,128)(2,1)}) %all-gather.31.cloned.1.call-update) | async-done | bytes 4718608 | tf_op jit(solution)/shard_map/all_gather | solution.py:53
  936.4 29.5 %convert_bitcast_fusion.1 = bf16[16,8,36,36,128]{4,1,0,3,2:T(8,128)(2,1)} fusion(bf16[1,512,128,36]{2,1,3,0:T(8,128)(2,1)} %param.10, bf16[1,512,36,128]{3,1,2,0:T(8,128)(2,1)} %all-gather.31.cloned.1.call-done), kind=kOutput, calls=%fused_computation.27 | convolution fusion | flops 21764505600 | bytes 51904512 | tf_op jit(solution)/shard_map/abm,asc->bmsc/dot_general | solution.py:56
  965.9 61.8 %all-gather.25.cloned.1.call-done = bf16[128,36,512]{2,0,1:T(8,128)(2,1)} async-done(((bf16[128,36,128]{2,0,1:T(8,128)(2,1)}), bf16[128,36,512]{2,0,1:T(8,128)(2,1)}) %all-gather.25.cloned.1.call-update) | async-done | bytes 4718608 | tf_op jit(solution)/shard_map/all_gather | solution.py:90
  1048.4 14.1 broadcast.9.clone2
  1062.6 220.8 %while.20 = (s32[]{:T(128)}, bf16[16,8,36,36,128]{4,1,0,3,2:T(8,128)(2,1)}, bf16[16,8,36,36,128]{4,1,0,3,2:T(8,128)(2,1)}, bf16[6,6,6,6,2]{1,3,4,0,2:T(8,128)(2,1)S(1)}, s32[]{:T(128)}) while((s32[]{:T(128)}, bf16[16,8,36,36,128]{4,1,0,3,2:T(8,128)(2,1)}, bf16[16,8,36,36,128]{4,1,0,3,2:T(8,128)(2,1)}, bf16[6,6,6,6,2]{1,3,4,0,2:T(8,128)(2,1)S(1)}, ...), condition=%wide.region_1.2_spmd, body=%wide.region_0.1_spmd.sunk | while | flops 386187264 | bytes 31861440 | solution.py:38
  1283.4 29.7 %fusion.32 = f32[512,36,128]{0,2,1:T(8,128)} fusion(bf16[128,36,512]{2,0,1:T(8,128)(2,1)} %all-gather.17.cloned.1.call-done, bf16[16,8,36,36,128]{4,1,0,3,2:T(8,128)(2,1)} %get-tuple-element.46), kind=kOutput, calls=%fused_computation.38 | convolution fusion | flops 21743271936 | bytes 56623104 | tf_op jit(solution)/shard_map/bmdc,bdk->kmc/dot_general | solution.py:63
  1319.5 14.8 all-gather.5
  1340.0 69.6 %reduce-scatter.4.cloned.1.call-done = f32[128,36,128]{0,2,1:T(8,128)} async-done(((f32[512,36,128]{0,2,1:T(8,128)}), f32[128,36,128]{0,2,1:T(8,128)}) %reduce-scatter.4.cloned.1.call-update) | async-done | bytes 2359312 | tf_op jit(solution)/shard_map/reduce_scatter | solution.py:62
  1412.6 87.6 %all-gather.29.cloned.1.call-done = bf16[128,36,512]{2,0,1:T(8,128)(2,1)} async-done(((bf16[128,36,128]{2,0,1:T(8,128)(2,1)}), bf16[128,36,512]{2,0,1:T(8,128)(2,1)}) %all-gather.29.cloned.1.call-update) | async-done | bytes 4718608 | tf_op jit(solution)/shard_map/all_gather | solution.py:90
  (220 shorter events, 551.2 us)
Async XLA Ops:
  7.2 355.6 %copy-start = (bf16[1,512,128]{2,1,0:T(8,128)(2,1)S(1)}, bf16[1,512,128]{2,1,0:T(8,128)(2,1)}, u32[]{:S(2)}) copy-start(bf16[1,512,128]{2,1,0:T(8,128)(2,1)} %param.14) | copy-start | bytes 393220
  7.2 62.5 %all-gather.33.cloned.1.call-start = ((), (), s32[]{:S(2)}) async-start(), calls=%async_computation.14 | async-start | bytes 5898240 | tf_op jit(solution)/shard_map/all_gather | solution.py:54
  7.9 516.3 %reduce-scatter.6.cloned.1.call-start = ((), (), s32[]{:S(2)}) async-start(), calls=%async_computation.5 | async-start | bytes 11796480 | tf_op jit(solution)/shard_map/reduce_scatter | solution.py:76
  362.7 184.8 %reduce-scatter.8.cloned.1.call-start = ((), (), s32[]{:S(2)}) async-start(), calls=%async_computation.7 | async-start | bytes 327680 | tf_op jit(solution)/shard_map/reduce_scatter | solution.py:77
  370.1 268.8 %all-gather.19.cloned.1.call-start = ((), (), s32[]{:S(2)}) async-start(), calls=%async_computation.6 | async-start | bytes 5898240 | tf_op jit(solution)/shard_map/all_gather | solution.py:80
  527.1 243.7 %all-gather.21.cloned.1.call-start = ((), (), s32[]{:S(2)}) async-start(), calls=%async_computation.8 | async-start | bytes 5898240 | tf_op jit(solution)/shard_map/all_gather | solution.py:90
  684.2 193.6 %all-gather.23.cloned.1.call-start = ((), (), s32[]{:S(2)}) async-start(), calls=%async_computation.9 | async-start | bytes 5898240 | tf_op jit(solution)/shard_map/all_gather | solution.py:90
  791.2 145.1 %all-gather.31.cloned.1.call-start = ((), (), s32[]{:S(2)}) async-start(), calls=%async_computation.13 | async-start | bytes 5898240 | tf_op jit(solution)/shard_map/all_gather | solution.py:53
  792.0 235.8 %all-gather.25.cloned.1.call-start = ((), (), s32[]{:S(2)}) async-start(), calls=%async_computation.10 | async-start | bytes 5898240 | tf_op jit(solution)/shard_map/all_gather | solution.py:90
  904.0 379.4 %all-gather.17.cloned.1.call-start = ((), (), s32[]{:S(2)}) async-start(), calls=%async_computation.3 | async-start | bytes 5898240 | tf_op jit(solution)/shard_map/all_gather | solution.py:61
  904.0 3.3 collective-permute-start
  907.3 406.1 %all-gather.27.cloned.1.call-start = ((), (), s32[]{:S(2)}) async-start(), calls=%async_computation.11 | async-start | bytes 5898240 | tf_op jit(solution)/shard_map/all_gather | solution.py:90
  1048.2 361.3 %reduce-scatter.4.cloned.1.call-start = ((), (), s32[]{:S(2)}) async-start(), calls=%async_computation.4 | async-start | bytes 11796480 | tf_op jit(solution)/shard_map/reduce_scatter | solution.py:62
  1313.1 1.7 copy-start.2
  1313.1 187.1 %all-gather.29.cloned.1.call-start = ((), (), s32[]{:S(2)}) async-start(), calls=%async_computation.12 | async-start | bytes 5898240 | tf_op jit(solution)/shard_map/all_gather | solution.py:90
  1339.9 160.2 %copy-start.3 = (f32[128,36,128]{2,0,1:T(8,128)S(1)}, f32[128,36,128]{2,0,1:T(8,128)}, u32[]{:S(2)}) copy-start(f32[128,36,128]{2,0,1:T(8,128)} %get-tuple-element.103) | copy-start | bytes 7077892
  1515.0 5.2 copy-start.1
Sparse Core Ops, SparseCore 0:
  9.9 59.7 all-gather.32
  362.8 161.2 reduce-scatter.5
  527.0 20.4 reduce-scatter.7
  549.6 89.1 all-gather.18
  684.3 86.4 all-gather.20
  791.3 86.3 all-gather.22
  879.8 56.5 all-gather.30
  938.6 89.1 all-gather.24
  1029.4 87.3 all-gather.16
  1118.8 87.3 all-gather.26
  1313.2 96.2 reduce-scatter.3
  1411.0 89.1 all-gather.28
